TPU v7x, 32 devices: a whole 2x2x4 slice. The times are simulated.
32 devices in a mesh: dp: 4 (over y, x), row: 2 (over core), col: 4 (over z).
Axes of the slice: x: 2, y: 2, z: 4, core: 2. Of those that a mesh axis runs over, the one named last changes fastest.
Arguments:
- inputs: bfloat16 [8192, 1536], P('dp', 'row'), may hold values from -6 to 6
- segments: int32 [4, 2048], P('dp'), may hold values from 0 to 5, never falling along the last dimension, each value on 1 to 1024 neighbouring positions
- cotangent: bfloat16 [8192, 1536], P('dp', 'row'), may hold values from -6 to 6
- norm_gain: float32 [1536], P('row'), may hold values from 0.1 to 1.9
- gate_proj: float32 [1536, 48, 64], P('dp', 'col', 'row'), may hold values from -0.15625 to 0.15625
- inner_proj: float32 [1536, 48, 64], P('dp', 'col', 'row'), may hold values from -0.15625 to 0.15625
- state_proj: float32 [1536, 256], P('dp'), may hold values from -0.15625 to 0.15625
- step_proj: float32 [1536, 48], P('dp', 'col'), may hold values from -0.15625 to 0.15625
- conv_inner: float32 [4, 48, 64], P(None, 'col', 'row'), may hold values from -0.5 to 0.5
- bias_inner: float32 [48, 64], P('col', 'row'), may hold values from -0.5 to 0.5
- conv_state: float32 [4, 256], replicated, may hold values from -0.5 to 0.5
- bias_state: float32 [256], replicated, may hold values from -0.5 to 0.5
- step_bias: float32 [48], P('col'), may hold values from -3 to -1
- decay_log: float32 [48], P('col'), may hold values from -2.3 to 1.4
- skip_gain: float32 [48], P('col'), may hold values from 0.25 to 1
- gate_norm: float32 [48, 64], P('col', 'row'), may hold values from 0.1 to 1.9
- out_proj: float32 [1536, 48, 64], P('dp', 'col', 'row'), may hold values from -0.109375 to 0.109375
Outputs:
- output: bfloat16 [8192, 1536], P('dp', 'row')
- grad_inputs: float32 [8192, 1536], P('dp', 'row')
- grad_norm_gain: float32 [1536], P('row')
- grad_gate_proj: float32 [1536, 48, 64], P('dp', 'col', 'row')
- grad_inner_proj: float32 [1536, 48, 64], P('dp', 'col', 'row')
- grad_state_proj: float32 [1536, 256], P('dp')
- grad_step_proj: float32 [1536, 48], P('dp', 'col')
- grad_conv_inner: float32 [4, 48, 64], P(None, 'col', 'row')
- grad_bias_inner: float32 [48, 64], P('col', 'row')
- grad_conv_state: float32 [4, 256], replicated
- grad_bias_state: float32 [256], replicated
- grad_step_bias: float32 [48], P('col')
- grad_decay_log: float32 [48], P('col')
- grad_skip_gain: float32 [48], P('col')
- grad_gate_norm: float32 [48, 64], P('col', 'row')
- grad_out_proj: float32 [1536, 48, 64], P('dp', 'col', 'row')
Inputs may be any that keep to these rules, and one draw needn't show every extreme that they name: `segments`: in each sequence the numbers never fall; a document is a run of equal numbers of at most 1024 tokens, and one document has exactly 1024.
All inputs are finite; a program needn't handle non-finite values.
Results may differ from a plain program's by a relative error of at most 0.012.
The roundings to bfloat16 on the way count: a program that leaves them out, or rounds other values in their place, can miss the bound.
Values may be sent and summed in bfloat16 or wider, within the bound.
A program may use at most 192 MiB of HBM per device.

v0:
```python
import jax
import jax.numpy as jnp
from jax import lax
from jax.sharding import PartitionSpec as P

H = 48
P_SIZE = 64
BLOCK_LEN = 256
EPSILON = 1e-05
HIGHEST = lax.Precision.HIGHEST


def conv_act(values, kernel, offset_bias, seg_ids):
    length = values.shape[0]
    width_k = kernel.shape[0]
    summed = offset_bias[None, :] + kernel[width_k - 1][None, :] * values
    for offset in range(1, width_k):
        shifted = jnp.pad(values, ((offset, 0), (0, 0)))[:length]
        earlier = jnp.pad(seg_ids, (offset, 0), constant_values=-1)[:length]
        within = (earlier == seg_ids).astype(jnp.float32)
        summed = summed + kernel[width_k - 1 - offset][None, :] * shifted * within[:, None]
    return jax.nn.silu(summed)


def ssm_gate(
    gate_pre, inner_act, state_act, step_size, decay_rate, skip_vals, seg_ids, head_count, block_len
):
    length = gate_pre.shape[0]
    channels = inner_act.shape[1] // head_count
    state_dim = state_act.shape[1] // 2
    block_count = length // block_len
    inner_heads = inner_act.reshape(length, head_count, channels)
    log_decay = step_size * decay_rate[None, :]
    cumul = jnp.cumsum(log_decay.reshape(block_count, block_len, head_count), axis=1)
    seg_blocks = seg_ids.reshape(block_count, block_len)
    driven = (inner_heads * step_size[:, :, None]).reshape(
        block_count, block_len, head_count, channels
    )
    in_blocks = state_act[:, :state_dim].reshape(block_count, block_len, state_dim)
    out_blocks = state_act[:, state_dim:].reshape(block_count, block_len, state_dim)
    positions = jnp.arange(block_len)
    causal = positions[:, None] >= positions[None, :]

    def intra_block(item):
        cum_block, seg_block, in_block, out_block, driven_block = item
        inner_prod = jnp.dot(out_block, in_block.T, precision=HIGHEST)
        gaps = cum_block.T[:, :, None] - cum_block.T[:, None, :]
        allowed = (causal & (seg_block[:, None] == seg_block[None, :]))[None]
        decays = jnp.where(allowed, jnp.exp(jnp.where(allowed, gaps, 0.0)), 0.0)
        mixing = decays * inner_prod[None]
        return jnp.einsum("hts,shp->thp", mixing, driven_block, precision=HIGHEST)

    local_out = lax.map(
        jax.checkpoint(intra_block), (cumul, seg_blocks, in_blocks, out_blocks, driven)
    )
    last_cum = cumul[:, -1, :]
    last_seg = seg_blocks[:, -1]
    tails = jnp.where(
        seg_blocks[:, :, None] == last_seg[:, None, None],
        jnp.exp(last_cum[:, None, :] - cumul),
        0.0,
    )
    contrib = jnp.einsum("kqhp,kqn->khpn", driven * tails[..., None], in_blocks, precision=HIGHEST)
    before_seg = jnp.concatenate([jnp.full((1,), -1, seg_ids.dtype), last_seg[:-1]])
    carried = (last_seg == before_seg).astype(jnp.float32)

    def advance(state, item):
        keep_flag, last_block, contrib_block = item
        renewed = keep_flag * jnp.exp(last_block)[:, None, None] * state + contrib_block
        return (renewed, state)

    initial = jnp.zeros((head_count, channels, state_dim), jnp.float32)
    final_state, entering = lax.scan(advance, initial, (carried, last_cum, contrib))
    reach = jnp.where(seg_blocks[:, :, None] == before_seg[:, None, None], jnp.exp(cumul), 0.0)
    from_state = (
        jnp.einsum("kqn,khpn->kqhp", out_blocks, entering, precision=HIGHEST) * reach[..., None]
    )
    mixed = (local_out + from_state).reshape(length, head_count, channels) + skip_vals[
        None, :, None
    ] * inner_heads
    gated = mixed * jax.nn.silu(gate_pre.reshape(length, head_count, channels))
    return gated.reshape(length, head_count * channels)


def contract_last(left, right):
    return lax.dot_general(
        left, right, (((1,), (1,)), ((), ())), preferred_element_type=jnp.float32
    )


def contract_first(left, right):
    return lax.dot_general(
        left, right, (((0,), (0,)), ((), ())), preferred_element_type=jnp.float32
    )


def per_device(
    inputs,
    segments,
    cotangent,
    norm_gain,
    gate_proj,
    inner_proj,
    state_proj,
    step_proj,
    conv_inner,
    bias_inner,
    conv_state,
    bias_state,
    step_bias,
    decay_log,
    skip_gain,
    gate_norm,
    out_proj,
):
    seg_ids = segments[0]
    length = inputs.shape[0]
    row_count = lax.axis_size("row")
    col_count = lax.axis_size("col")
    row_at = lax.axis_index("row")
    col_at = lax.axis_index("col")
    group_size = row_count * col_count
    model_width = inputs.shape[1] * row_count
    head_count = gate_proj.shape[1]
    channels = gate_proj.shape[2]
    local_width = head_count * channels
    state_width = state_proj.shape[1]
    pieces = model_width // group_size
    member = row_at * col_count + col_at
    state_share = state_width // group_size
    half_heads = head_count // row_count
    inner_width = H * P_SIZE
    plain = inputs.astype(jnp.float32)
    sq_total = lax.psum(jnp.sum(plain * plain, axis=1), "row")
    scaling = lax.rsqrt(sq_total / model_width + EPSILON)
    normed_half = (plain * scaling[:, None] * norm_gain[None, :]).astype(jnp.bfloat16)
    normed = lax.all_gather(normed_half, "row", axis=1, tiled=True)
    gathered = (
        lax.all_gather(gate_proj.astype(jnp.bfloat16), "dp", axis=0, tiled=True),
        lax.all_gather(inner_proj.astype(jnp.bfloat16), "dp", axis=0, tiled=True),
        lax.all_gather(state_proj.astype(jnp.bfloat16), "dp", axis=0, tiled=True),
        lax.all_gather(step_proj.astype(jnp.bfloat16), "dp", axis=0, tiled=True),
        lax.all_gather(out_proj.astype(jnp.bfloat16), "dp", axis=0, tiled=True),
    )
    gate_w = gathered[0].reshape(model_width, local_width)
    inner_w = gathered[1].reshape(model_width, local_width)
    state_w = gathered[2]
    step_w = gathered[3]
    out_w = gathered[4].reshape(model_width, local_width)
    gate_pre = jnp.dot(normed, gate_w, preferred_element_type=jnp.float32)
    inner_pre = jnp.dot(normed, inner_w, preferred_element_type=jnp.float32)
    state_pre = jnp.dot(normed, state_w, preferred_element_type=jnp.float32)
    step_pre = jnp.dot(normed, step_w, preferred_element_type=jnp.float32)
    step_arg = step_pre + step_bias[None, :]
    step_size = jax.nn.softplus(step_arg)
    decay_rate = -jnp.exp(decay_log)

    def state_conv(pre_vals, kernel, offset_bias):
        return conv_act(pre_vals, kernel, offset_bias, seg_ids)

    state_act, state_back = jax.vjp(state_conv, state_pre, conv_state, bias_state)

    def mixer(
        gate_vals, inner_vals, state_vals, step_vals, decay_vals, skip_vals, kernel, offset_bias
    ):
        inner_act = conv_act(inner_vals, kernel, offset_bias, seg_ids)
        return ssm_gate(
            gate_vals,
            inner_act,
            state_vals,
            step_vals,
            decay_vals,
            skip_vals,
            seg_ids,
            head_count,
            BLOCK_LEN,
        )

    gated, mixer_back = jax.vjp(
        mixer,
        gate_pre,
        inner_pre,
        state_act,
        step_size,
        decay_rate,
        skip_gain,
        conv_inner.reshape(conv_inner.shape[0], local_width),
        bias_inner.reshape(local_width),
    )
    gsum = lax.psum(jnp.sum(gated * gated, axis=1), ("row", "col"))
    gate_scale = lax.rsqrt(gsum / inner_width + EPSILON)
    gain_flat = gate_norm.reshape(local_width)
    normed_gate = (gated * gate_scale[:, None] * gain_flat[None, :]).astype(jnp.bfloat16)
    partial_out = contract_last(normed_gate, out_w)
    out_slice = lax.psum_scatter(partial_out, ("row", "col"), scatter_dimension=1, tiled=True)
    plain_slice = lax.dynamic_slice_in_dim(plain, col_at * pieces, pieces, 1)
    out_rows = (plain_slice + out_slice).astype(jnp.bfloat16)
    output = lax.all_gather(out_rows, "col", axis=1, tiled=True)
    cot_full = lax.all_gather(cotangent, "row", axis=1, tiled=True)
    d_normed_gate = jnp.dot(cot_full, out_w, preferred_element_type=jnp.float32)
    grad_out = contract_first(cot_full, normed_gate)
    grad_gate_gain = jnp.sum(d_normed_gate * gated * gate_scale[:, None], axis=0)
    weighted = d_normed_gate * gain_flat[None, :]
    gate_dot = lax.psum(jnp.sum(weighted * gated, axis=1), ("row", "col"))
    d_gated = (
        gate_scale[:, None] * weighted - gated * (gate_scale**3 * gate_dot / inner_width)[:, None]
    )
    d_gate_pre, d_inner_pre, d_state_act, d_step, d_decay, d_skip, d_conv_in, d_bias_in = (
        mixer_back(d_gated)
    )
    wide_heads = head_count * col_count
    wide_step = lax.dynamic_update_slice_in_dim(
        jnp.zeros((length, wide_heads), jnp.float32), d_step, col_at * head_count, 1
    )
    wide_decay = lax.dynamic_update_slice_in_dim(
        jnp.zeros((wide_heads,), jnp.float32), d_decay, col_at * head_count, 0
    )
    wide_skip = lax.dynamic_update_slice_in_dim(
        jnp.zeros((wide_heads,), jnp.float32), d_skip, col_at * head_count, 0
    )
    shared = lax.psum((d_state_act, wide_step, wide_decay, wide_skip), ("row", "col"))
    d_state_full = shared[0]
    d_step_full = lax.dynamic_slice_in_dim(shared[1], col_at * head_count, head_count, 1)
    d_decay_full = lax.dynamic_slice_in_dim(shared[2], col_at * head_count, head_count, 0)
    d_skip_full = lax.dynamic_slice_in_dim(shared[3], col_at * head_count, head_count, 0)
    d_state_pre, grad_conv_st, grad_bias_st = state_back(d_state_full)
    d_step_arg = d_step_full * jax.nn.sigmoid(step_arg)
    grad_step_bias = jnp.sum(d_step_arg, axis=0)
    grad_decay = d_decay_full * decay_rate
    gate_low = d_gate_pre.astype(jnp.bfloat16)
    inner_low = d_inner_pre.astype(jnp.bfloat16)
    state_low = d_state_pre.astype(jnp.bfloat16)
    step_low = d_step_arg.astype(jnp.bfloat16)
    state_part = contract_last(
        lax.dynamic_slice_in_dim(state_low, member * state_share, state_share, 1),
        lax.dynamic_slice_in_dim(state_w, member * state_share, state_share, 1),
    )
    step_part = contract_last(
        lax.dynamic_slice_in_dim(step_low, row_at * half_heads, half_heads, 1),
        lax.dynamic_slice_in_dim(step_w, row_at * half_heads, half_heads, 1),
    )
    d_normed = (
        contract_last(gate_low, gate_w) + contract_last(inner_low, inner_w) + state_part + step_part
    )
    grad_gate_w = contract_first(normed, gate_low)
    grad_inner_w = contract_first(normed, inner_low)
    grad_state_w = contract_first(normed, state_low)
    grad_step_w = contract_first(normed, step_low)
    cot_plain = cotangent.astype(jnp.float32)
    d_half = lax.psum_scatter(d_normed, "row", scatter_dimension=1, tiled=True)
    d_half = lax.psum(d_half, "col")
    weighted_in = d_half * norm_gain[None, :]
    input_dot = lax.psum(jnp.sum(weighted_in * plain, axis=1), "row")
    grad_rows = (
        cot_plain
        + scaling[:, None] * weighted_in
        - plain * (scaling**3 * input_dot / model_width)[:, None]
    )
    grad_norm = jnp.sum(d_half * plain * scaling[:, None], axis=0)
    big = (
        lax.psum_scatter(
            grad_gate_w.reshape(model_width, head_count, channels),
            "dp",
            scatter_dimension=0,
            tiled=True,
        ),
        lax.psum_scatter(
            grad_inner_w.reshape(model_width, head_count, channels),
            "dp",
            scatter_dimension=0,
            tiled=True,
        ),
        lax.psum_scatter(grad_state_w, "dp", scatter_dimension=0, tiled=True),
        lax.psum_scatter(grad_step_w, "dp", scatter_dimension=0, tiled=True),
        lax.psum_scatter(
            grad_out.reshape(model_width, head_count, channels),
            "dp",
            scatter_dimension=0,
            tiled=True,
        ),
    )
    small = lax.psum(
        (
            grad_norm,
            d_conv_in.reshape(conv_inner.shape),
            d_bias_in.reshape(bias_inner.shape),
            grad_conv_st,
            grad_bias_st,
            grad_step_bias,
            grad_decay,
            d_skip_full,
            grad_gate_gain.reshape(gate_norm.shape),
        ),
        "dp",
    )
    return (
        output,
        grad_rows,
        small[0],
        big[0],
        big[1],
        big[2],
        big[3],
        small[1],
        small[2],
        small[3],
        small[4],
        small[5],
        small[6],
        small[7],
        small[8],
        big[4],
    )


def solution(mesh):
    return jax.shard_map(
        per_device,
        mesh=mesh,
        in_specs=(
            P("dp", "row"),
            P("dp", None),
            P("dp", "row"),
            P("row"),
            P("dp", "col", "row"),
            P("dp", "col", "row"),
            P("dp", None),
            P("dp", "col"),
            P(None, "col", "row"),
            P("col", "row"),
            P(),
            P(),
            P("col"),
            P("col"),
            P("col"),
            P("col", "row"),
            P("dp", "col", "row"),
        ),
        out_specs=(
            P("dp", "row"),
            P("dp", "row"),
            P("row"),
            P("dp", "col", "row"),
            P("dp", "col", "row"),
            P("dp", None),
            P("dp", "col"),
            P(None, "col", "row"),
            P("col", "row"),
            P(),
            P(),
            P("col"),
            P("col"),
            P("col"),
            P("col", "row"),
            P("dp", "col", "row"),
        ),
        check_vma=False,
    )
```

profile of v0, /device:TPU:0, one launch (start us, length us, event | category | flops | bytes accessed | tf_op | source)
XLA Modules:
  0.0 1333.0 jit_solution(18420000439808059908)
XLA Ops:
  23.6 10.2 all_gather.26
  33.9 14.0 %all_gather.27 = bf16[1536,256]{1,0:T(8,128)(2,1)} all-gather(bf16[384,256]{1,0:T(8,128)(2,1)S(1)} %convert_element_type.83), channel_id=1, replica_groups=mesh['dp'=4,'row'=2,'col'=4] {'dp'}, dimensions={0}, use_global_device_ids=true | all-gather | bytes 983040 | tf_op jit(solution)/shard_map/all_gather | solution.py:141
  50.5 11.6 all-gather.7.cloned.1.call-done
  110.1 54.1 %while.72 = (s32[]{:T(128)}, f32[12,32,128]{2,1,0:T(8,128)S(1)}, f32[8,12,32,128]{3,2,1,0:T(8,128)}, f32[8,12]{1,0:T(8,128)}, f32[8,12,1,1]{1,3,2,0:T(1,128)}, /...) while((s32[]{:T(128)}, f32[12,32,128]{2,1,0:T(8,128)S(1)}, ...), condition=%wide.region_7.8_spmd.clone, body=%wide.region_6.7_spmd.clone.sunk | while | flops 196635 | bytes 985236 | solution.py:73
  172.3 57.1 %while.70 = (s32[]{:T(128)}, f32[8,256,12,32]{1,3,2,0:T(8,128)}, f32[8,256,12,32]{1,3,2,0:T(8,128)S(1)}, s32[8,256]{1,0:T(8,128)}, f32[8,256,12]{1,2,0:T(8,128)}...) while((s32[]{:T(128)}, f32[8,256,12,32]{1,3,2,0:T(8,128)}, ...), condition=%wide.region_5.6_spmd.clone, body=%wide.region_4.5_spmd.clone.sunk | while | flops 405995520 | bytes 1766501 | solution.py:53
  236.3 9.7 multiply_reduce_fusion.9
  246.0 17.5 %psum.127 = f32[2048]{0:T(1024)S(1)} all-reduce(f32[2048]{0:T(1024)S(1)} %get-tuple-element.940), channel_id=1, replica_groups=mesh['dp'=4,'row'=2,'col'=4] {'row','col'}, use_global_device_ids=true, to_apply=%region_9.10 | all-reduce | flops 2048 | bytes 16384 | tf_op jit(solution)/shard_map/psum | solution.py:190
  263.6 8.1 fusion.84
  271.6 14.0 %psum.128 = f32[2048]{0:T(1024)S(1)} all-reduce(f32[2048]{0:T(1024)S(1)} %get-tuple-element.834), channel_id=1, replica_groups=mesh['dp'=4,'row'=2,'col'=4] {'row','col'}, use_global_device_ids=true, to_apply=%region_12.13 | all-reduce | flops 2048 | bytes 16384 | tf_op jit(solution)/shard_map/psum | solution.py:204
  304.5 114.0 %while.71 = (s32[]{:T(128)}, f32[8,256,12]{1,2,0:T(8,128)S(1)}, f32[8,256,128]{2,1,0:T(8,128)}, f32[8,256,128]{2,1,0:T(8,128)}, f32[8,256,12,32]{1,3,2,0:T(8,128...) while((s32[]{:T(128)}, f32[8,256,12]{1,2,0:T(8,128)S(1)}, ...), condition=%wide.region_20.21_spmd.clone, body=%wide.region_16.20_spmd.clone.sunk | while | flops 917897216 | bytes 6503601 | solution.py:53
  419.8 36.3 %while.73 = (s32[]{:T(128)}, f32[12,32,128]{2,1,0:T(8,128)S(1)}, f32[8,12]{1,0:T(8,128)S(1)}, f32[8,12,32,128]{3,2,1,0:T(8,128)}, f32[8,12,32,128]{3,2,1,0:T(8,1...) while((s32[]{:T(128)}, f32[12,32,128]{2,1,0:T(8,128)S(1)}, ...), condition=%wide.region_15.16_spmd.clone, body=%wide.region_13.15_spmd.clone.sunk | while | flops 294928 | bytes 1180264 | solution.py:73
  456.1 8.1 fusion.117
  464.3 7.7 fusion.120
  484.5 19.9 %reduce-window.16 = f32[8,12,2,128]{3,1,2,0:T(8,128)S(1)} reduce-window(f32[8,12,2,128]{3,1,2,0:T(8,128)S(1)} %copy.159, f32[]{:T(128)} %constant.213.clone.1), window={size=1x1x1x128 pad=0_0x0_0x0_0x0_127}, to_apply=%region_26.27 | reduce-window | flops 3121152 | bytes 196612 | tf_op jit(solution)/shard_map/reduce-window.2
  511.3 7.8 convolution_bitcast_fusion.2
  523.5 9.5 multiply_reduce_fusion.5
  541.8 6.5 fusion.160
  548.2 31.2 %all-reduce.34.cloned.1.call-done = (f32[2048,256]{1,0:T(8,128)}, f32[2048,48]{0,1:T(8,128)}) async-done(((f32[2048,256]{1,0:T(8,128)}, f32[2048,48]{0,1:T(8,128)}), (f32[2048,256]{1,0:T(8,128)}, f32[2048,48]{0,1:T(8,128)})) %all-reduce.34.cloned.1.call-update) | async-done | bytes 2490384 | tf_op jit(solution)/shard_map/psum | solution.py:221
  593.6 17.8 %fusion.60 = f32[2048,1536]{1,0:T(8,128)} fusion(f32[2048,1536]{1,0:T(8,128)} %fusion.126, f32[2048,1536]{1,0:T(8,128)} %fusion.161, f32[2048,1536,1]{1,0,2:T(8,128)} %fusion.160, bf16[2048,12]{0,1:T(8,128)(2,1)S(1)} %get-tuple-element.937, s32[]{:T(128)S(6)} %select_n.96, bf16[1536,12]{0,1:T(8,128)(2,1)S(1)} %copy-done.50), kind=kOutput, calls=%fused_computation.77 | convolution fusion | flops 47185920 | bytes 50390016 | tf_op jit(solution)/shard_map/dot_general | solution.py:86
  616.5 210.1 %reduce-scatter.22.cloned.1.call-done = f32[192,2048]{1,0:T(8,128)} async-done(((f32[1536,2048]{1,0:T(8,128)}), f32[192,2048]{1,0:T(8,128)}) %reduce-scatter.22.cloned.1.call-update) | async-done | bytes 1572880
  835.9 15.8 %reduce-scatter.10.cloned.1.call-done = f32[2048,768]{1,0:T(8,128)} async-done(((f32[2048,1536]{1,0:T(8,128)}), f32[2048,768]{1,0:T(8,128)}) %reduce-scatter.10.cloned.1.call-update) | async-done | bytes 6291472 | tf_op jit(solution)/shard_map/reduce_scatter | solution.py:250
  862.3 7.6 fusion.68
  870.0 7.3 fusion.162
  877.4 7.3 fusion.165
  885.5 18.0 %all-reduce.26 = (f32[48]{0:T(128)S(1)}, f32[48]{0:T(128)S(1)}) all-reduce(f32[48]{0:T(128)S(1)} %dynamic_update_slice.85, f32[48]{0:T(128)S(1)} %dynamic_update_slice.86), channel_id=1, replica_groups=mesh['dp'=4,'row'=2,'col'=4] {'row','col'}, use_global_device_ids=true, to_apply=%region_56.57 | all-reduce | flops 96 | bytes 768 | tf_op jit(solution)/shard_map/psum | solution.py:221
  903.7 15.4 %all-gather.15.cloned.1.call-done = bf16[2048,768]{0,1:T(8,128)(2,1)} async-done(((bf16[2048,192]{0,1:T(8,128)(2,1)}), bf16[2048,768]{0,1:T(8,128)(2,1)}) %all-gather.15.cloned.1.call-update) | async-done | bytes 3145744 | tf_op jit(solution)/shard_map/all_gather | solution.py:198
  923.6 219.5 %all-reduce.32.cloned.1.call-done = f32[2048,768]{1,0:T(8,128)} async-done(((f32[2048,768]{1,0:T(8,128)}), f32[2048,768]{1,0:T(8,128)}) %all-reduce.32.cloned.1.call-update) | async-done | bytes 6291472 | tf_op jit(solution)/shard_map/psum | solution.py:251
  1147.3 17.6 %all-reduce.28 = (f32[768]{0:T(1024)}, f32[4,12,32]{2,1,0:T(8,128)S(1)}, f32[12,32]{1,0:T(8,128)}, f32[4,256]{1,0:T(4,128)}, f32[256]{0:T(256)}, /*index=5*/f32[...) all-reduce(f32[768]{0:T(1024)S(1)} %get-tuple-element.831, ...), channel_id=1, replica_groups=mesh['dp'=4,'row'=2,'col'=4] {'dp'}, use_global_device_ids=true, to_apply=%region_34.35 | all-reduce | flops 4388 | bytes 35104 | tf_op jit(solution)/shard_map/psum | solution.py:282
  1174.2 29.1 %reduce-scatter.16.cloned.1.call-done = f32[384,256]{1,0:T(8,128)} async-done(((f32[1536,256]{1,0:T(8,128)}), f32[384,256]{1,0:T(8,128)}) %reduce-scatter.16.cloned.1.call-update) | async-done | bytes 393232 | tf_op jit(solution)/shard_map/reduce_scatter | solution.py:273
  1203.2 41.0 %reduce-scatter.12.cloned.1.call-done = f32[384,12,32]{0,2,1:T(8,128)} async-done(((f32[1536,12,32]{0,2,1:T(8,128)}), f32[384,12,32]{0,2,1:T(8,128)}) %reduce-scatter.12.cloned.1.call-update) | async-done | bytes 589840 | tf_op jit(solution)/shard_map/reduce_scatter | solution.py:261
  1244.3 40.9 %reduce-scatter.14.cloned.1.call-done = f32[384,12,32]{0,2,1:T(8,128)} async-done(((f32[1536,12,32]{0,2,1:T(8,128)}), f32[384,12,32]{0,2,1:T(8,128)}) %reduce-scatter.14.cloned.1.call-update) | async-done | bytes 589840 | tf_op jit(solution)/shard_map/reduce_scatter | solution.py:267
  1285.2 40.9 %reduce-scatter.20.cloned.1.call-done = f32[384,12,32]{0,2,1:T(8,128)} async-done(((f32[1536,12,32]{0,2,1:T(8,128)}), f32[384,12,32]{0,2,1:T(8,128)}) %reduce-scatter.20.cloned.1.call-update) | async-done | bytes 589840 | tf_op jit(solution)/shard_map/reduce_scatter | solution.py:275
  (613 shorter events, 452.0 us)
Async XLA Ops:
  7.2 43.3 %all-gather.9.cloned.1.call-start = ((), (), s32[]{:S(2)}) async-start(), calls=%async_computation.8 | async-start | bytes 1474560 | tf_op jit(solution)/shard_map/all_gather | solution.py:140
  9.2 52.9 %all-gather.7.cloned.1.call-start = ((), (), s32[]{:S(2)}) async-start(), calls=%async_computation.7 | async-start | bytes 9437184 | tf_op jit(solution)/shard_map/all_gather | solution.py:137
  17.7 218.7 %all-gather.11.cloned.1.call-start = ((), (), s32[]{:S(2)}) async-start(), calls=%async_computation.9 | async-start | bytes 1474560 | tf_op jit(solution)/shard_map/all_gather | solution.py:139
  19.4 30.5 %copy-start.59 = (f32[12,32]{1,0:T(8,128)S(1)}, f32[12,32]{1,0:T(8,128)}, u32[]{:S(2)}) copy-start(f32[12,32]{1,0:T(8,128)} %param.40) | copy-start | bytes 4612
  19.4 244.1 %all-gather.13.cloned.1.call-start = ((), (), s32[]{:S(2)}) async-start(), calls=%async_computation.10 | async-start | bytes 1474560 | tf_op jit(solution)/shard_map/all_gather | solution.py:143
  20.2 243.3 %all-gather.17.cloned.1.call-start = ((), (), s32[]{:S(2)}) async-start(), calls=%async_computation.12 | async-start | bytes 9437184 | tf_op jit(solution)/shard_map/all_gather | solution.py:199
  20.8 558.6 %all-reduce.34.cloned.1.call-start = ((), (), s32[]{:S(2)}) async-start(), calls=%async_computation.21 | async-start | bytes 4980736 | tf_op jit(solution)/shard_map/psum | solution.py:221
  22.1 45.9 %copy-start.51 = (s32[8,256]{1,0:T(8,128)}, s32[8,256]{1,0:T(8,128)S(1)}, u32[]{:S(2)}) copy-start(s32[8,256]{1,0:T(8,128)S(1)} %reshape_squeeze.2) | copy-start | bytes 24580
  22.6 45.4 %copy-start.45 = (f32[2048]{0:T(1024)}, f32[2048]{0:T(1024)S(1)}, u32[]{:S(2)}) copy-start(f32[2048]{0:T(1024)S(1)} %get-tuple-element.976) | copy-start | bytes 24580
  22.7 45.3 %copy-start.70 = (f32[384]{0:T(512)}, f32[384]{0:T(512)S(1)}, u32[]{:S(2)}) copy-start(f32[384]{0:T(512)S(1)} %mul.739) | copy-start | bytes 4612
  22.8 45.2 %copy-start.72 = (f32[384]{0:T(512)}, f32[384]{0:T(512)S(1)}, u32[]{:S(2)}) copy-start(f32[384]{0:T(512)S(1)} %mul.734) | copy-start | bytes 4612
  22.9 45.1 %copy-start.74 = (f32[384]{0:T(512)}, f32[384]{0:T(512)S(1)}, u32[]{:S(2)}) copy-start(f32[384]{0:T(512)S(1)} %mul.729) | copy-start | bytes 4612
  23.0 45.1 %copy-start.76 = (f32[384]{0:T(512)}, f32[384]{0:T(512)S(1)}, u32[]{:S(2)}) copy-start(f32[384]{0:T(512)S(1)} %mul.721) | copy-start | bytes 4612
  172.3 57.2 %copy-start.28 = (f32[8,256,12]{1,2,0:T(8,128)S(1)}, f32[8,256,12]{1,2,0:T(8,128)}, u32[]{:S(2)}) copy-start(f32[8,256,12]{1,2,0:T(8,128)} %get-tuple-element.970) | copy-start | bytes 294916
  246.0 39.7 %copy-start.11 = (f32[2048,12,32]{0,2,1:T(8,128)}, f32[2048,12,32]{0,2,1:T(8,128)S(1)}, u32[]{:S(2)}) copy-start(f32[2048,12,32]{0,2,1:T(8,128)S(1)} %get-tuple-element.941) | copy-start | bytes 9437188
  304.5 115.3 %copy-start.98 = (f32[8]{0:T(128)S(1)}, f32[8]{0:T(128)}, u32[]{:S(2)}) copy-start(f32[8]{0:T(128)} %get-tuple-element.1435) | copy-start | bytes 100
  419.8 44.4 %copy-start.27 = (f32[8,256,12]{1,2,0:T(8,128)S(1)}, f32[8,256,12]{1,2,0:T(8,128)}, u32[]{:S(2)}) copy-start(f32[8,256,12]{1,2,0:T(8,128)} %copy-done.26) | copy-start | bytes 294916
  511.2 315.3 %reduce-scatter.22.cloned.1.call-start = ((), (), s32[]{:S(2)}) async-start(), calls=%async_computation.20 | async-start | bytes 14155776
  519.1 332.6 %reduce-scatter.10.cloned.1.call-start = ((), (), s32[]{:S(2)}) async-start(), calls=%async_computation.13 | async-start | bytes 18874368 | tf_op jit(solution)/shard_map/reduce_scatter | solution.py:250
  541.7 37.7 %copy-start.36 = (f32[2,8,8,256]{3,1,2,0:T(8,128)S(1)}, f32[2,8,8,256]{3,1,2,0:T(8,128)}, u32[]{:S(2)}) copy-start(f32[2,8,8,256]{3,1,2,0:T(8,128)} %copy-done.35) | copy-start | bytes 393220
  541.7 37.7 %copy-start.39 = (f32[2048,12]{0,1:T(8,128)S(1)}, f32[2048,12]{0,1:T(8,128)}, u32[]{:S(2)}) copy-start(f32[2048,12]{0,1:T(8,128)} %get-tuple-element.981) | copy-start | bytes 294916
  541.8 38.8 %copy-start.20 = (f32[2048,256]{1,0:T(8,128)S(1)}, f32[2048,256]{1,0:T(8,128)}, u32[]{:S(2)}) copy-start(f32[2048,256]{1,0:T(8,128)} %copy-done.19) | copy-start | bytes 6291460
  611.4 307.6 %all-gather.15.cloned.1.call-start = ((), (), s32[]{:S(2)}) async-start(), calls=%async_computation.11 | async-start | bytes 3932160 | tf_op jit(solution)/shard_map/all_gather | solution.py:198
  835.9 307.2 %all-reduce.32.cloned.1.call-start = ((), (), s32[]{:S(2)}) async-start(), calls=%async_computation.14 | async-start | bytes 12582912 | tf_op jit(solution)/shard_map/psum | solution.py:251
  851.7 322.5 %reduce-scatter.18.cloned.1.call-start = ((), (), s32[]{:S(2)}) async-start(), calls=%async_computation.18 | async-start | bytes 122880 | tf_op jit(solution)/shard_map/reduce_scatter | solution.py:274
  856.1 347.1 %reduce-scatter.16.cloned.1.call-start = ((), (), s32[]{:S(2)}) async-start(), calls=%async_computation.17 | async-start | bytes 1966080 | tf_op jit(solution)/shard_map/reduce_scatter | solution.py:273
  862.3 382.0 %reduce-scatter.12.cloned.1.call-start = ((), (), s32[]{:S(2)}) async-start(), calls=%async_computation.15 | async-start | bytes 2949120 | tf_op jit(solution)/shard_map/reduce_scatter | solution.py:261
  870.0 415.2 %reduce-scatter.14.cloned.1.call-start = ((), (), s32[]{:S(2)}) async-start(), calls=%async_computation.16 | async-start | bytes 2949120 | tf_op jit(solution)/shard_map/reduce_scatter | solution.py:267
  877.3 448.8 %reduce-scatter.20.cloned.1.call-start = ((), (), s32[]{:S(2)}) async-start(), calls=%async_computation.19 | async-start | bytes 2949120 | tf_op jit(solution)/shard_map/reduce_scatter | solution.py:275
  903.6 239.5 %copy-start.53 = (f32[2048]{0:T(1024)S(1)}, f32[2048]{0:T(1024)}, u32[]{:S(2)}) copy-start(f32[2048]{0:T(1024)} %copy-done.52) | copy-start | bytes 24580
  903.7 239.5 %copy-start.62 = (f32[768]{0:T(1024)S(1)}, f32[768]{0:T(1024)}, u32[]{:S(2)}) copy-start(f32[768]{0:T(1024)} %param.28) | copy-start | bytes 9220
  923.6 244.3 %copy-start.58 = (f32[2048]{0:T(1024)S(1)}, f32[2048]{0:T(1024)}, u32[]{:S(2)}) copy-start(f32[2048]{0:T(1024)} %copy-done.57) | copy-start | bytes 24580
  (90 other events, 516.8 us)
Sparse Core Ops, SparseCore 0:
  10.4 32.6 all-gather.8
  45.3 16.8 all-gather.6
  64.5 28.7 all-gather.10
  95.5 27.5 all-gather.12
  124.5 16.7 all-gather.16
  511.4 68.0 all-reduce.33
  581.8 244.6 reduce-scatter.21
  829.0 22.6 reduce-scatter.9
  853.9 65.0 all-gather.14
  921.4 221.7 all-reduce.31
  1146.6 22.1 reduce-scatter.17
  1172.3 30.9 reduce-scatter.15
  1206.9 37.3 reduce-scatter.11
  1247.8 37.3 reduce-scatter.13
  1288.7 37.3 reduce-scatter.19
where the time goes:
time: 1350 us; the launch traced here: 1330 us
  waiting for transfers between devices  656 us (49%)
  matrix products  274 us (20%)
  other arithmetic  165 us (12%)
  local copies, waits for them, and re-layouts  124 us (9%)
  blocking collectives  96.5 us (7%)
  between operations  15.6 us (1%)
    psum x1, waiting for transfers between devices, per_device(): d_half = lax.psum(d_half, 'col')  219 us
    unnamed x16, waiting for transfers between devices  211 us
    dot_general x24, matrix products, intra_block(): return jnp.einsum('hts,shp->thp', mixing, driven_block, precision=HIGHEST)  95.9 us
    dot_general x5, matrix products, contract_last(): lax.dot_general(left, right, (((1,), (1,)), ((), ())), preferred_element_...  44.8 us
    reduce_scatter x1, waiting for transfers between devices, per_device(): lax.psum_scatter(grad_gate_w.reshape(model_width, head_count, channels),...  41 us
    reduce_scatter x1, waiting for transfers between devices, per_device(): lax.psum_scatter(grad_inner_w.reshape(model_width, head_count, channels),...  40.9 us
    reduce_scatter x1, waiting for transfers between devices, per_device(): lax.psum_scatter(grad_out.reshape(model_width, head_count, channels), 'dp...  40.9 us
    dot_general x5, matrix products, contract_first(): lax.dot_general(left, right, (((0,), (0,)), ((), ())), preferred_element_...  32.7 us
  transfers between devices with their start and end apart: 15, of which 10 were waited for; matrix products, arithmetic and copies ran while one was open for 24% of the time, Pallas kernels for 0%

commit v1 on v0

--- a/solution.py
+++ b/solution.py
@@ -8,6 +8,12 @@
 BLOCK_LEN = 256
 EPSILON = 1e-05
 HIGHEST = lax.Precision.HIGHEST
+
+
+def run_blocks(vector, named_axis, chip_axis):
+    for nth in (named_axis, chip_axis):
+        vector = lax.psum(vector, nth)
+    return vector
 
 
 def conv_act(values, kernel, offset_bias, seg_ids):
@@ -218,7 +224,7 @@
     wide_skip = lax.dynamic_update_slice_in_dim(
         jnp.zeros((wide_heads,), jnp.float32), d_skip, col_at * head_count, 0
     )
-    shared = lax.psum((d_state_act, wide_step, wide_decay, wide_skip), ("row", "col"))
+    shared = run_blocks((d_state_act, wide_step, wide_decay, wide_skip), "col", "row")
     d_state_full = shared[0]
     d_step_full = lax.dynamic_slice_in_dim(shared[1], col_at * head_count, head_count, 1)
     d_decay_full = lax.dynamic_slice_in_dim(shared[2], col_at * head_count, head_count, 0)

time: 1350 us -> 1400 us (1.037)
  waiting for transfers between devices: 656 us -> 718 us
    psum x1 -> x2, waiting for transfers between devices: 31.2 us -> 100 us  [run_blocks(): vector = lax.psum(vector, nth)]
    reduce_scatter x1, waiting for transfers between devices: 41 us -> 8.33 us  [per_device(): lax.psum_scatter(grad_gate_w.reshape(model_width, head_count, channels),...]
    reduce_scatter x1, waiting for transfers between devices: 0.01 us -> 26.6 us  [per_device(): lax.psum_scatter(grad_step_w, 'dp', scatter_dimension=0, tiled=True)]
    unnamed x16 -> x17, waiting for transfers between devices: 211 us -> 198 us
  transfers between devices with their start and end apart: 15 -> 16, of which waited for: 10 -> 11; matrix products, arithmetic and copies ran while one was open for 24% -> 23% of each run, Pallas kernels for 0% -> 0%
where the time goes in v1:
time: 1400 us; the launch traced here: 1390 us
  waiting for transfers between devices  718 us (51%)
  matrix products  274 us (20%)
  other arithmetic  164 us (12%)
  local copies, waits for them, and re-layouts  124 us (9%)
  blocking collectives  92.8 us (7%)
  between operations  15.6 us (1%)
    psum x1, waiting for transfers between devices, per_device(): d_half = lax.psum(d_half, 'col')  219 us
    unnamed x17, waiting for transfers between devices  198 us
    psum x2, waiting for transfers between devices, run_blocks(): vector = lax.psum(vector, nth)  100 us
    dot_general x24, matrix products, intra_block(): return jnp.einsum('hts,shp->thp', mixing, driven_block, precision=HIGHEST)  95.9 us
    dot_general x5, matrix products, contract_last(): lax.dot_general(left, right, (((1,), (1,)), ((), ())), preferred_element_...  45 us
    reduce_scatter x1, waiting for transfers between devices, per_device(): lax.psum_scatter(grad_inner_w.reshape(model_width, head_count, channels),...  41.3 us
    reduce_scatter x1, waiting for transfers between devices, per_device(): lax.psum_scatter(grad_out.reshape(model_width, head_count, channels), 'dp...  41.2 us
    reduce_scatter x1, waiting for transfers between devices, per_device(): lax.psum_scatter(grad_state_w, 'dp', scatter_dimension=0, tiled=True)  34.4 us
  transfers between devices with their start and end apart: 16, of which 11 were waited for; matrix products, arithmetic and copies ran while one was open for 23% of the time, Pallas kernels for 0%

profile of v1, /device:TPU:0, one launch (start us, length us, event | category | flops | bytes accessed | tf_op | source)
XLA Modules:
  0.0 1390.8 jit_solution(13683185534554640422)
XLA Ops:
  23.6 10.3 all_gather.26
  33.9 14.0 %all_gather.27 = bf16[1536,256]{1,0:T(8,128)(2,1)} all-gather(bf16[384,256]{1,0:T(8,128)(2,1)S(1)} %convert_element_type.83), channel_id=1, replica_groups=mesh['dp'=4,'row'=2,'col'=4] {'dp'}, dimensions={0}, use_global_device_ids=true | all-gather | bytes 983040 | tf_op jit(solution)/shard_map/all_gather | solution.py:147
  50.4 11.7 all-gather.7.cloned.1.call-done
  110.1 53.9 %while.72 = (s32[]{:T(128)}, f32[12,32,128]{2,1,0:T(8,128)S(1)}, f32[8,12,32,128]{3,2,1,0:T(8,128)}, f32[8,12]{1,0:T(8,128)}, f32[8,12,1,1]{1,3,2,0:T(1,128)}, /...) while((s32[]{:T(128)}, f32[12,32,128]{2,1,0:T(8,128)S(1)}, ...), condition=%wide.region_7.8_spmd.clone, body=%wide.region_6.7_spmd.clone.sunk | while | flops 196635 | bytes 985236 | solution.py:79
  172.1 57.1 %while.70 = (s32[]{:T(128)}, f32[8,256,12,32]{1,3,2,0:T(8,128)}, f32[8,256,12,32]{1,3,2,0:T(8,128)S(1)}, s32[8,256]{1,0:T(8,128)}, f32[8,256,12]{1,2,0:T(8,128)}...) while((s32[]{:T(128)}, f32[8,256,12,32]{1,3,2,0:T(8,128)}, ...), condition=%wide.region_5.6_spmd.clone, body=%wide.region_4.5_spmd.clone.sunk | while | flops 405995520 | bytes 1766501 | solution.py:59
  236.2 9.7 multiply_reduce_fusion.9
  245.8 17.5 %psum.155 = f32[2048]{0:T(1024)S(1)} all-reduce(f32[2048]{0:T(1024)S(1)} %get-tuple-element.945), channel_id=1, replica_groups=mesh['dp'=4,'row'=2,'col'=4] {'row','col'}, use_global_device_ids=true, to_apply=%region_9.10 | all-reduce | flops 2048 | bytes 16384 | tf_op jit(solution)/shard_map/psum | solution.py:196
  263.4 8.1 fusion.84
  271.5 14.0 %psum.156 = f32[2048]{0:T(1024)S(1)} all-reduce(f32[2048]{0:T(1024)S(1)} %get-tuple-element.834), channel_id=1, replica_groups=mesh['dp'=4,'row'=2,'col'=4] {'row','col'}, use_global_device_ids=true, to_apply=%region_12.13 | all-reduce | flops 2048 | bytes 16384 | tf_op jit(solution)/shard_map/psum | solution.py:210
  304.4 114.0 %while.71 = (s32[]{:T(128)}, f32[8,256,12]{1,2,0:T(8,128)S(1)}, f32[8,256,128]{2,1,0:T(8,128)}, f32[8,256,128]{2,1,0:T(8,128)}, f32[8,256,12,32]{1,3,2,0:T(8,128...) while((s32[]{:T(128)}, f32[8,256,12]{1,2,0:T(8,128)S(1)}, ...), condition=%wide.region_20.21_spmd.clone, body=%wide.region_16.20_spmd.clone.sunk | while | flops 917897216 | bytes 6503601 | solution.py:59
  419.7 36.3 %while.73 = (s32[]{:T(128)}, f32[12,32,128]{2,1,0:T(8,128)S(1)}, f32[8,12]{1,0:T(8,128)S(1)}, f32[8,12,32,128]{3,2,1,0:T(8,128)}, f32[8,12,32,128]{3,2,1,0:T(8,1...) while((s32[]{:T(128)}, f32[12,32,128]{2,1,0:T(8,128)S(1)}, ...), condition=%wide.region_15.16_spmd.clone, body=%wide.region_13.15_spmd.clone.sunk | while | flops 294928 | bytes 1180264 | solution.py:79
  456.1 8.1 fusion.117
  464.2 7.7 fusion.120
  484.6 19.9 %reduce-window.16 = f32[8,12,2,128]{3,1,2,0:T(8,128)S(1)} reduce-window(f32[8,12,2,128]{3,1,2,0:T(8,128)S(1)} %copy.159, f32[]{:T(128)} %constant.213.clone.1), window={size=1x1x1x128 pad=0_0x0_0x0_0x0_127}, to_apply=%region_27.28 | reduce-window | flops 3121152 | bytes 196612 | tf_op jit(solution)/shard_map/reduce-window.2
  509.8 100.3 %all-reduce.37.cloned.1.call-done = (f32[2048,256]{1,0:T(8,128)}, f32[2048,48]{0,1:T(8,128)}) async-done(((f32[2048,256]{1,0:T(8,128)}, f32[2048,48]{0,1:T(8,128)}), (f32[2048,256]{1,0:T(8,128)}, f32[2048,48]{0,1:T(8,128)})) %all-reduce.37.cloned.1.call-update) | async-done | bytes 2490384 | tf_op jit(solution)/shard_map/psum | solution.py:15
  610.2 8.0 convolution_bitcast_fusion.2
  622.6 10.3 multiply_reduce_fusion.5
  662.1 17.9 %fusion.60 = f32[2048,1536]{1,0:T(8,128)} fusion(f32[2048,1536]{1,0:T(8,128)} %fusion.126, f32[2048,1536]{1,0:T(8,128)} %fusion.161, f32[2048,1536,1]{1,0,2:T(8,128)} %fusion.160, bf16[2048,12]{0,1:T(8,128)(2,1)S(1)} %get-tuple-element.942, s32[]{:T(128)S(6)} %select_n.96, bf16[1536,12]{0,1:T(8,128)(2,1)S(1)} %copy-done.52), kind=kOutput, calls=%fused_computation.77 | convolution fusion | flops 47185920 | bytes 50390016 | tf_op jit(solution)/shard_map/dot_general | solution.py:92
  685.0 197.7 %reduce-scatter.22.cloned.1.call-done = f32[192,2048]{1,0:T(8,128)} async-done(((f32[1536,2048]{1,0:T(8,128)}), f32[192,2048]{1,0:T(8,128)}) %reduce-scatter.22.cloned.1.call-update) | async-done | bytes 1572880
  892.1 15.8 %reduce-scatter.10.cloned.1.call-done = f32[2048,768]{1,0:T(8,128)} async-done(((f32[2048,1536]{1,0:T(8,128)}), f32[2048,768]{1,0:T(8,128)}) %reduce-scatter.10.cloned.1.call-update) | async-done | bytes 6291472 | tf_op jit(solution)/shard_map/reduce_scatter | solution.py:256
  907.9 7.2 fusion.68
  915.2 7.5 fusion.162
  922.8 7.3 fusion.165
  941.5 12.3 all-reduce.26
  953.8 21.0 %all-gather.15.cloned.1.call-done = bf16[2048,768]{0,1:T(8,128)(2,1)} async-done(((bf16[2048,192]{0,1:T(8,128)(2,1)}), bf16[2048,768]{0,1:T(8,128)(2,1)}) %all-gather.15.cloned.1.call-update) | async-done | bytes 3145744 | tf_op jit(solution)/shard_map/all_gather | solution.py:204
  979.5 219.4 %all-reduce.35.cloned.1.call-done = f32[2048,768]{1,0:T(8,128)} async-done(((f32[2048,768]{1,0:T(8,128)}), f32[2048,768]{1,0:T(8,128)}) %all-reduce.35.cloned.1.call-update) | async-done | bytes 6291472 | tf_op jit(solution)/shard_map/psum | solution.py:257
  1205.7 19.5 %all-reduce.28 = (f32[768]{0:T(1024)}, f32[4,12,32]{2,1,0:T(8,128)S(1)}, f32[12,32]{1,0:T(8,128)}, f32[4,256]{1,0:T(4,128)}, f32[256]{0:T(256)}, /*index=5*/f32[...) all-reduce(f32[768]{0:T(1024)S(1)} %get-tuple-element.831, ...), channel_id=1, replica_groups=mesh['dp'=4,'row'=2,'col'=4] {'dp'}, use_global_device_ids=true, to_apply=%region_36.37 | all-reduce | flops 4388 | bytes 35104 | tf_op jit(solution)/shard_map/psum | solution.py:288
  1232.1 8.3 reduce-scatter.12.cloned.1.call-done
  1240.4 41.3 %reduce-scatter.14.cloned.1.call-done = f32[384,12,32]{0,2,1:T(8,128)} async-done(((f32[1536,12,32]{0,2,1:T(8,128)}), f32[384,12,32]{0,2,1:T(8,128)}) %reduce-scatter.14.cloned.1.call-update) | async-done | bytes 589840 | tf_op jit(solution)/shard_map/reduce_scatter | solution.py:273
  1281.7 41.2 %reduce-scatter.20.cloned.1.call-done = f32[384,12,32]{0,2,1:T(8,128)} async-done(((f32[1536,12,32]{0,2,1:T(8,128)}), f32[384,12,32]{0,2,1:T(8,128)}) %reduce-scatter.20.cloned.1.call-update) | async-done | bytes 589840 | tf_op jit(solution)/shard_map/reduce_scatter | solution.py:281
  1322.9 26.6 %reduce-scatter.18.cloned.1.call-done = f32[384,12]{0,1:T(8,128)} async-done(((f32[1536,12]{0,1:T(8,128)}), f32[384,12]{0,1:T(8,128)}) %reduce-scatter.18.cloned.1.call-update) | async-done | bytes 18448 | tf_op jit(solution)/shard_map/reduce_scatter | solution.py:280
  1349.5 34.4 %reduce-scatter.16.cloned.1.call-done = f32[384,256]{1,0:T(8,128)} async-done(((f32[1536,256]{1,0:T(8,128)}), f32[384,256]{1,0:T(8,128)}) %reduce-scatter.16.cloned.1.call-update) | async-done | bytes 393232 | tf_op jit(solution)/shard_map/reduce_scatter | solution.py:279
  (620 shorter events, 456.9 us)
Async XLA Ops:
  7.2 43.2 %all-gather.9.cloned.1.call-start = ((), (), s32[]{:S(2)}) async-start(), calls=%async_computation.8 | async-start | bytes 1474560 | tf_op jit(solution)/shard_map/all_gather | solution.py:146
  9.2 52.9 %all-gather.7.cloned.1.call-start = ((), (), s32[]{:S(2)}) async-start(), calls=%async_computation.7 | async-start | bytes 9437184 | tf_op jit(solution)/shard_map/all_gather | solution.py:143
  17.7 218.5 %all-gather.11.cloned.1.call-start = ((), (), s32[]{:S(2)}) async-start(), calls=%async_computation.9 | async-start | bytes 1474560 | tf_op jit(solution)/shard_map/all_gather | solution.py:145
  19.4 30.4 %copy-start.61 = (f32[12,32]{1,0:T(8,128)S(1)}, f32[12,32]{1,0:T(8,128)}, u32[]{:S(2)}) copy-start(f32[12,32]{1,0:T(8,128)} %param.40) | copy-start | bytes 4612
  19.4 244.0 %all-gather.13.cloned.1.call-start = ((), (), s32[]{:S(2)}) async-start(), calls=%async_computation.10 | async-start | bytes 1474560 | tf_op jit(solution)/shard_map/all_gather | solution.py:149
  20.2 243.1 %all-gather.17.cloned.1.call-start = ((), (), s32[]{:S(2)}) async-start(), calls=%async_computation.12 | async-start | bytes 9437184 | tf_op jit(solution)/shard_map/all_gather | solution.py:205
  20.8 589.2 %all-reduce.37.cloned.1.call-start = ((), (), s32[]{:S(2)}) async-start(), calls=%async_computation.21 | async-start | bytes 4980736 | tf_op jit(solution)/shard_map/psum | solution.py:15
  22.1 45.9 %copy-start.53 = (s32[8,256]{1,0:T(8,128)}, s32[8,256]{1,0:T(8,128)S(1)}, u32[]{:S(2)}) copy-start(s32[8,256]{1,0:T(8,128)S(1)} %reshape_squeeze.2) | copy-start | bytes 24580
  22.6 45.4 %copy-start.47 = (f32[2048]{0:T(1024)}, f32[2048]{0:T(1024)S(1)}, u32[]{:S(2)}) copy-start(f32[2048]{0:T(1024)S(1)} %get-tuple-element.981) | copy-start | bytes 24580
  22.7 45.3 %copy-start.72 = (f32[384]{0:T(512)}, f32[384]{0:T(512)S(1)}, u32[]{:S(2)}) copy-start(f32[384]{0:T(512)S(1)} %mul.739) | copy-start | bytes 4612
  22.8 45.2 %copy-start.74 = (f32[384]{0:T(512)}, f32[384]{0:T(512)S(1)}, u32[]{:S(2)}) copy-start(f32[384]{0:T(512)S(1)} %mul.734) | copy-start | bytes 4612
  22.9 45.1 %copy-start.76 = (f32[384]{0:T(512)}, f32[384]{0:T(512)S(1)}, u32[]{:S(2)}) copy-start(f32[384]{0:T(512)S(1)} %mul.729) | copy-start | bytes 4612
  23.0 45.0 %copy-start.78 = (f32[384]{0:T(512)}, f32[384]{0:T(512)S(1)}, u32[]{:S(2)}) copy-start(f32[384]{0:T(512)S(1)} %mul.721) | copy-start | bytes 4612
  172.1 57.2 %copy-start.30 = (f32[8,256,12]{1,2,0:T(8,128)S(1)}, f32[8,256,12]{1,2,0:T(8,128)}, u32[]{:S(2)}) copy-start(f32[8,256,12]{1,2,0:T(8,128)} %get-tuple-element.975) | copy-start | bytes 294916
  245.8 39.8 %copy-start.11 = (f32[2048,12,32]{0,2,1:T(8,128)}, f32[2048,12,32]{0,2,1:T(8,128)S(1)}, u32[]{:S(2)}) copy-start(f32[2048,12,32]{0,2,1:T(8,128)S(1)} %get-tuple-element.946) | copy-start | bytes 9437188
  304.4 115.3 %copy-start.100 = (f32[8]{0:T(128)S(1)}, f32[8]{0:T(128)}, u32[]{:S(2)}) copy-start(f32[8]{0:T(128)} %get-tuple-element.1450) | copy-start | bytes 100
  419.7 44.5 %copy-start.29 = (f32[8,256,12]{1,2,0:T(8,128)S(1)}, f32[8,256,12]{1,2,0:T(8,128)}, u32[]{:S(2)}) copy-start(f32[8,256,12]{1,2,0:T(8,128)} %copy-done.28) | copy-start | bytes 294916
  506.6 103.6 %copy-start.12 = (f32[2048,12,32]{0,2,1:T(8,128)S(1)}, f32[2048,12,32]{0,2,1:T(8,128)}, u32[]{:S(2)}) copy-start(f32[2048,12,32]{0,2,1:T(8,128)} %copy-done.11) | copy-start | bytes 9437188
  509.7 138.3 %all-reduce.39.cloned.1.call-start = ((), (), s32[]{:S(2)}) async-start(), calls=%async_computation.22 | async-start | bytes 4980736 | tf_op jit(solution)/shard_map/psum | solution.py:15
  610.1 272.6 %reduce-scatter.22.cloned.1.call-start = ((), (), s32[]{:S(2)}) async-start(), calls=%async_computation.20 | async-start | bytes 14155776
  618.2 289.7 %reduce-scatter.10.cloned.1.call-start = ((), (), s32[]{:S(2)}) async-start(), calls=%async_computation.13 | async-start | bytes 18874368 | tf_op jit(solution)/shard_map/reduce_scatter | solution.py:256
  679.9 294.9 %all-gather.15.cloned.1.call-start = ((), (), s32[]{:S(2)}) async-start(), calls=%async_computation.11 | async-start | bytes 3932160 | tf_op jit(solution)/shard_map/all_gather | solution.py:204
  892.0 306.9 %all-reduce.35.cloned.1.call-start = ((), (), s32[]{:S(2)}) async-start(), calls=%async_computation.14 | async-start | bytes 12582912 | tf_op jit(solution)/shard_map/psum | solution.py:257
  907.9 332.5 %reduce-scatter.12.cloned.1.call-start = ((), (), s32[]{:S(2)}) async-start(), calls=%async_computation.15 | async-start | bytes 2949120 | tf_op jit(solution)/shard_map/reduce_scatter | solution.py:267
  915.2 366.5 %reduce-scatter.14.cloned.1.call-start = ((), (), s32[]{:S(2)}) async-start(), calls=%async_computation.16 | async-start | bytes 2949120 | tf_op jit(solution)/shard_map/reduce_scatter | solution.py:273
  922.8 400.1 %reduce-scatter.20.cloned.1.call-start = ((), (), s32[]{:S(2)}) async-start(), calls=%async_computation.19 | async-start | bytes 2949120 | tf_op jit(solution)/shard_map/reduce_scatter | solution.py:281
  930.2 419.3 %reduce-scatter.18.cloned.1.call-start = ((), (), s32[]{:S(2)}) async-start(), calls=%async_computation.18 | async-start | bytes 122880 | tf_op jit(solution)/shard_map/reduce_scatter | solution.py:280
  934.6 449.2 %reduce-scatter.16.cloned.1.call-start = ((), (), s32[]{:S(2)}) async-start(), calls=%async_computation.17 | async-start | bytes 1966080 | tf_op jit(solution)/shard_map/reduce_scatter | solution.py:279
  953.8 245.1 %copy-start.55 = (f32[2048]{0:T(1024)S(1)}, f32[2048]{0:T(1024)}, u32[]{:S(2)}) copy-start(f32[2048]{0:T(1024)} %copy-done.54) | copy-start | bytes 24580
  953.8 245.1 %copy-start.64 = (f32[768]{0:T(1024)S(1)}, f32[768]{0:T(1024)}, u32[]{:S(2)}) copy-start(f32[768]{0:T(1024)} %param.28) | copy-start | bytes 9220
  979.5 226.2 %copy-start.99 = (f32[12]{0:T(128)S(1)}, f32[12]{0:T(128)}, u32[]{:S(2)}) copy-start(f32[12]{0:T(128)} %param.38) | copy-start | bytes 148
  979.5 246.3 %copy-start.60 = (f32[2048]{0:T(1024)S(1)}, f32[2048]{0:T(1024)}, u32[]{:S(2)}) copy-start(f32[2048]{0:T(1024)} %copy-done.59) | copy-start | bytes 24580
  (93 other events, 545.7 us)
Sparse Core Ops, SparseCore 0:
  10.4 32.6 all-gather.8
  45.3 16.8 all-gather.6
  64.5 28.7 all-gather.10
  95.5 27.5 all-gather.12
  124.5 16.7 all-gather.16
  509.9 100.1 all-reduce.36
  612.5 21.0 all-reduce.38
  635.9 246.7 reduce-scatter.21
  885.1 22.7 reduce-scatter.9
  909.9 64.8 all-gather.14
  977.3 221.4 all-reduce.34
  1202.7 37.6 reduce-scatter.11
  1244.3 37.3 reduce-scatter.13
  1285.5 37.3 reduce-scatter.19
  1326.3 23.1 reduce-scatter.17
  1352.9 30.8 reduce-scatter.15
